TPU v7x, 32 devices: a whole 2x2x4 slice. The times are simulated.
32 devices in a mesh: ctx: 16 (over z, y, core), ch: 2 (over x).
Axes of the slice: x: 2, y: 2, z: 4, core: 2. Of those that a mesh axis runs over, the one named last changes fastest.
Arguments:
- inputs: float32 [12288, 2048], P('ctx', 'ch'), may hold values from -6 to 6
- cotangent: float32 [12288, 2048], P('ctx', 'ch'), may hold values from -6 to 6
- filter_rows: float32 [1536, 2048], P('ctx', 'ch'), may hold values from -0.15625 to 0.15625
- skip_gain: float32 [2048], P('ch'), may hold values from -1 to 1
- band_blocks: int32 [2048], P('ch'), may hold values from 1 to 2
Outputs:
- outputs: float32 [12288, 2048], P('ctx', 'ch')
- input_grad: float32 [2048, 12288], P(('ch', 'ctx'))
All inputs are finite; a program needn't handle non-finite values.
Results may differ from a plain program's by a relative error of at most 0.00007.
Values sent between devices are 32-bit elements; how exact they have to be, the bound alone decides.
A program may use at most 192 MiB of HBM per device.

v0:
```python
import math
import jax
import jax.numpy as jnp
from jax import lax
from jax.sharding import PartitionSpec as P

PRECISE = lax.Precision.HIGHEST


def passed_along(value, axis, steps):
    count = lax.axis_size(axis)
    initial, last = (max(0, -steps), min(count, count - steps))
    return lax.ppermute(value, axis, [(source, source + steps) for source in range(initial, last)])


def factor_pair(length):
    leading = 1
    candidate = 1
    while candidate * candidate <= length:
        if length % candidate == 0:
            leading = candidate
        candidate += 1
    return (leading, length // leading)


def twiddle_table(row_count, col_count, period, direction):
    product = (
        jnp.arange(row_count, dtype=jnp.int32)[:, None]
        * jnp.arange(col_count, dtype=jnp.int32)[None, :]
        % period
    )
    angle_val = product.astype(jnp.float32) * (2.0 * math.pi / period)
    return (jnp.cos(angle_val), direction * jnp.sin(angle_val))


def forward_real(signal, factors):
    leading, trailing = factors
    length = leading * trailing
    kept = trailing // 2 + 1
    grid_view = signal.reshape(leading, trailing, signal.shape[-1])
    cos_first, sin_first = twiddle_table(leading, leading, leading, -1.0)
    section_real = jnp.einsum("kn,nmc->kmc", cos_first, grid_view, precision=PRECISE)
    section_imag = jnp.einsum("kn,nmc->kmc", sin_first, grid_view, precision=PRECISE)
    turn_real, turn_imag = twiddle_table(leading, trailing, length, -1.0)
    rot_real = section_real * turn_real[:, :, None] - section_imag * turn_imag[:, :, None]
    rot_imag = section_real * turn_imag[:, :, None] + section_imag * turn_real[:, :, None]
    cos_second, sin_second = twiddle_table(trailing, kept, trailing, -1.0)
    out_real = jnp.einsum("kmc,mj->kjc", rot_real, cos_second, precision=PRECISE) - jnp.einsum(
        "kmc,mj->kjc", rot_imag, sin_second, precision=PRECISE
    )
    out_imag = jnp.einsum("kmc,mj->kjc", rot_real, sin_second, precision=PRECISE) + jnp.einsum(
        "kmc,mj->kjc", rot_imag, cos_second, precision=PRECISE
    )
    return jnp.stack([out_real, out_imag])


def inverse_real(spectrum, factors, channel_major):
    leading, trailing = factors
    length = leading * trailing
    kept = trailing // 2 + 1
    freq_index = (
        jnp.arange(leading, dtype=jnp.int32)[:, None]
        + leading * jnp.arange(kept, dtype=jnp.int32)[None, :]
    )
    edge_bin = (freq_index == 0) | (2 * freq_index == length)
    weights = jnp.where(edge_bin, 1.0, jnp.where(2 * freq_index < length, 2.0, 0.0)).astype(
        jnp.float32
    )
    spec_real = spectrum[0] * weights[:, :, None]
    spec_imag = spectrum[1] * weights[:, :, None]
    cos_second, sin_second = twiddle_table(kept, trailing, trailing, 1.0)
    part_real = jnp.einsum("kjc,jm->kmc", spec_real, cos_second, precision=PRECISE) - jnp.einsum(
        "kjc,jm->kmc", spec_imag, sin_second, precision=PRECISE
    )
    part_imag = jnp.einsum("kjc,jm->kmc", spec_real, sin_second, precision=PRECISE) + jnp.einsum(
        "kjc,jm->kmc", spec_imag, cos_second, precision=PRECISE
    )
    turn_real, turn_imag = twiddle_table(leading, trailing, length, 1.0)
    rot_real = part_real * turn_real[:, :, None] - part_imag * turn_imag[:, :, None]
    rot_imag = part_real * turn_imag[:, :, None] + part_imag * turn_real[:, :, None]
    cos_first, sin_first = twiddle_table(leading, leading, leading, 1.0)
    if channel_major:
        result = jnp.einsum("nk,kmc->cnm", cos_first, rot_real, precision=PRECISE) - jnp.einsum(
            "nk,kmc->cnm", sin_first, rot_imag, precision=PRECISE
        )
        return result.reshape(result.shape[0], length) / length
    result = jnp.einsum("nk,kmc->nmc", cos_first, rot_real, precision=PRECISE) - jnp.einsum(
        "nk,kmc->nmc", sin_first, rot_imag, precision=PRECISE
    )
    return result.reshape(length, result.shape[-1]) / length


def spectral_product(tap_spec, panel_spec, conjugate):
    tap_real, tap_imag = (tap_spec[0], tap_spec[1])
    if conjugate:
        tap_imag = -tap_imag
    panel_real, panel_imag = (panel_spec[0], panel_spec[1])
    return jnp.stack(
        [
            tap_real * panel_real - tap_imag * panel_imag,
            tap_real * panel_imag + tap_imag * panel_real,
        ]
    )


def local(inputs, cotangent, filter_rows, skip_gain, band_blocks):
    block_len = inputs.shape[0]
    factors = factor_pair(2 * block_len)
    piece_rows = lax.all_gather(filter_rows, "ctx", axis=0, tiled=True)
    lag_index = jnp.arange(piece_rows.shape[0], dtype=jnp.int32)
    keep_mask = lag_index[:, None] < band_blocks[None, :] * block_len
    filter_full = jnp.where(keep_mask, piece_rows, jnp.zeros_like(piece_rows))
    lag_zero = jnp.arange(filter_full.shape[0], dtype=jnp.int32)[:, None] == 0
    filter_full = filter_full + jnp.where(lag_zero, skip_gain[None, :], 0.0)
    blank_rows = jnp.zeros_like(inputs)
    lower_one = passed_along(inputs, "ctx", 1)
    upper_one = passed_along(cotangent, "ctx", -1)
    own_forward = forward_real(jnp.concatenate([lower_one, inputs], axis=0), factors)
    own_backward = forward_real(jnp.concatenate([cotangent, upper_one], axis=0), factors)
    forward_sources = [own_forward]
    backward_sources = [own_backward]
    lag_block = 1
    forward_sources.append(passed_along(own_forward, "ctx", lag_block))
    backward_sources.append(passed_along(own_backward, "ctx", -lag_block))

    def tile_terms(totals, lag_block):
        tap_block = lax.slice_in_dim(
            filter_full, lag_block * block_len, (lag_block + 1) * block_len, axis=0
        )
        tap_spec = forward_real(jnp.concatenate([tap_block, blank_rows], axis=0), factors)
        forward_panel = forward_sources[lag_block]
        backward_panel = backward_sources[lag_block]
        return (
            totals[0] + spectral_product(tap_spec, forward_panel, False),
            totals[1] + spectral_product(tap_spec, backward_panel, True),
        )

    totals = tile_terms((0.0, 0.0), 0)
    lag_block = 1
    totals = tile_terms(totals, lag_block)
    forward_time = inverse_real(totals[0], factors, False)
    outputs = lax.slice_in_dim(forward_time, block_len, 2 * block_len, axis=0)
    backward_time = inverse_real(totals[1], factors, True)
    local_grad = lax.slice_in_dim(backward_time, 0, block_len, axis=1)
    input_grad = lax.all_to_all(local_grad, "ctx", split_axis=0, concat_axis=1, tiled=True)
    return (outputs, input_grad)


def solution(mesh):
    return jax.shard_map(
        local,
        mesh=mesh,
        in_specs=(P("ctx", "ch"), P("ctx", "ch"), P("ctx", "ch"), P("ch"), P("ch")),
        out_specs=(P("ctx", "ch"), P(("ch", "ctx"), None)),
        check_vma=False,
    )
```

profile of v0, /device:TPU:0, one launch (start us, length us, event | category | flops | bytes accessed | tf_op | source)
XLA Modules:
  0.0 702.1 jit_solution(13089642921306606010)
XLA Ops:
  19.7 10.0 %fusion.44 = f32[32,48,1024]{2,0,1:T(8,128)} fusion(f32[32,48,1024]{2,1,0:T(8,128)S(1)} %bitcast.317), kind=kOutput, calls=%fused_computation.69 | convolution fusion | flops 603995136 | bytes 12582912 | tf_op jit(solution)/shard_map/kn,nmc->kmc/dot_general | solution.py:43
  29.7 10.1 %fusion.46 = f32[32,48,1024]{2,0,1:T(8,128)} fusion(f32[32,48,1024]{2,1,0:T(8,128)S(1)} %bitcast.318), kind=kOutput, calls=%fused_computation.71 | convolution fusion | flops 603994112 | bytes 12582912 | tf_op jit(solution)/shard_map/kn,nmc->kmc/dot_general | solution.py:42
  39.8 10.3 %fusion.22 = f32[32,48,1024]{2,0,1:T(8,128)} fusion(f32[32,48,1024]{2,1,0:T(8,128)S(1)} %bitcast.303), kind=kOutput, calls=%fused_computation.47 | convolution fusion | flops 603994112 | bytes 12582912 | tf_op jit(solution)/shard_map/kn,nmc->kmc/dot_general | solution.py:42
  50.1 53.3 %all-gather.2.cloned.1.call-done = f32[1536,1024]{1,0:T(8,128)} async-done(((f32[96,1024]{1,0:T(8,128)}), f32[1536,1024]{1,0:T(8,128)}) %all-gather.2.cloned.1.call-update) | async-done | bytes 6291472 | tf_op jit(solution)/shard_map/all_gather | solution.py:109
  108.7 10.1 %fusion.32 = f32[32,48,1024]{2,0,1:T(8,128)} fusion(f32[32,48,1024]{2,1,0:T(8,128)S(1)} %bitcast.315), kind=kOutput, calls=%fused_computation.57 | convolution fusion | flops 603995136 | bytes 12582912 | tf_op jit(solution)/shard_map/kn,nmc->kmc/dot_general | solution.py:43
  118.7 10.4 %fusion.34 = f32[32,48,1024]{2,0,1:T(8,128)} fusion(f32[32,48,1024]{2,1,0:T(8,128)S(1)} %bitcast.316), kind=kOutput, calls=%fused_computation.59 | convolution fusion | flops 603994112 | bytes 12582912 | tf_op jit(solution)/shard_map/kn,nmc->kmc/dot_general | solution.py:42
  129.2 10.1 %fusion.56 = f32[32,48,1024]{2,0,1:T(8,128)} fusion(f32[32,48,1024]{2,1,0:T(8,128)S(1)} %bitcast.313), kind=kOutput, calls=%fused_computation.81 | convolution fusion | flops 603995136 | bytes 12582912 | tf_op jit(solution)/shard_map/kn,nmc->kmc/dot_general | solution.py:43
  139.2 10.3 %fusion.58 = f32[32,48,1024]{2,0,1:T(8,128)} fusion(f32[32,48,1024]{2,1,0:T(8,128)S(1)} %bitcast.314), kind=kOutput, calls=%fused_computation.83 | convolution fusion | flops 603994112 | bytes 12582912 | tf_op jit(solution)/shard_map/kn,nmc->kmc/dot_general | solution.py:42
  149.5 40.5 %multiply_subtract_fusion = (f32[32,48,1024]{2,0,1:T(8,128)}, f32[32,48,1024]{2,0,1:T(8,128)}, f32[32,48,1024]{2,0,1:T(8,128)}, f32[32,48,1024]{2,0,1:T(8,128)},...) fusion(f32[32,48,1024]{2,0,1:T(8,128)} %fusion.22, ...), kind=kOutput, calls=%fused_computation.28 | convolution fusion | flops 641743872 | bytes 100675584 | tf_op jit(solution)/shard_map/kn,nmc->kmc/dot_general | solution.py:43
  190.1 10.7 %fusion.12 = f32[25,32,1024]{2,0,1:T(8,128)S(1)} fusion(f32[32,48,1024]{2,0,1:T(8,128)} %get-tuple-element.13), kind=kOutput, calls=%fused_computation.37 | convolution fusion | flops 471870016 | bytes 9568256 | tf_op jit(solution)/shard_map/kmc,mj->kjc/dot_general | solution.py:51
  209.1 8.6 %fusion.38 = f32[25,32,1024]{2,0,1:T(8,128)} fusion(f32[32,48,1024]{2,0,1:T(8,128)S(1)} %bitcast.306), kind=kOutput, calls=%fused_computation.63 | convolution fusion | flops 471871200 | bytes 9568256 | tf_op jit(solution)/shard_map/kmc,mj->kjc/dot_general | solution.py:48
  247.0 10.3 %copy.136 = f32[2,32,25,1024]{3,1,2,0:T(8,128)} copy(f32[2,32,25,1024]{3,2,1,0:T(8,128)} %pad_maximum_fusion.1) | data formatting | bytes 13107200 | tf_op jit(solution)/shard_map/stack | solution.py:54
  266.7 8.8 %fusion.124 = f32[25,32,1024]{2,0,1:T(8,128)} fusion(f32[25,32,1024]{2,0,1:T(8,128)S(1)} %fusion.36, f32[32,48,1024]{2,0,1:T(8,128)S(1)} %bitcast.296), kind=kOutput, calls=%fused_computation.153 | convolution fusion | flops 472690400 | bytes 12845056 | tf_op jit(solution)/shard_map/kmc,mj->kjc/dot_general | solution.py:51
  282.6 9.9 %copy.120 = f32[2,32,25,1024]{3,1,2,0:T(8,128)} copy(f32[2,32,25,1024]{3,2,1,0:T(8,128)} %pad_maximum_fusion) | data formatting | bytes 13107200 | tf_op jit(solution)/shard_map/stack | solution.py:54
  292.5 36.6 %collective-permute-start.1 = (f32[2,32,25,1024]{3,1,2,0:T(8,128)}, f32[2,32,25,1024]{3,1,2,0:T(8,128)}, u32[]{:S(2)}, u32[]{:S(2)}) collective-permute-start(f32[2,32,25,1024]{3,1,2,0:T(8,128)} %copy.120), channel_id=1, source_target_pairs={{0,2},{2,4},{4,6},{6,8},{8,10},{10,12},{12,14},{14,16},{16,18},{18... | collective-permute-start | bytes 19660808 | tf_op jit(solution)/shard_map/ppermute | solution.py:13
  337.3 8.5 %fusion.50 = f32[25,32,1024]{2,0,1:T(8,128)} fusion(f32[32,48,1024]{2,0,1:T(8,128)S(1)} %bitcast.302), kind=kOutput, calls=%fused_computation.75 | convolution fusion | flops 471871200 | bytes 9568256 | tf_op jit(solution)/shard_map/kmc,mj->kjc/dot_general | solution.py:48
  353.9 8.5 %fusion.26 = f32[25,32,1024]{2,0,1:T(8,128)} fusion(f32[32,48,1024]{2,0,1:T(8,128)S(1)} %bitcast.300), kind=kOutput, calls=%fused_computation.51 | convolution fusion | flops 471871200 | bytes 9568256 | tf_op jit(solution)/shard_map/kmc,mj->kjc/dot_general | solution.py:48
  379.1 19.3 %fusion.81 = (f32[1,32,25,1024]{3,2,1,0:T(8,128)}, f32[1,32,25,1024]{3,2,1,0:T(8,128)}, f32[1,32,25,1024]{3,2,1,0:T(8,128)}, f32[1,32,25,1024]{3,2,1,0:T(8,128)}) fusion(f32[25,32,1024]{2,0,1:T(8,128)S(1)} %fusion.136, f32[25,32,1024]{2,0,1:T(8,128)} %copy-done.3, f32[25,32,1024]{2,0,1:T(8,128)} %fusion.118, f32[25,32,1024]{2,0,1:T(8,128)} %copy-done.4, ...), kind=kOutput, calls=%fused_computation.116 | convolution fusion | flops 483338816 | bytes 39059456 | tf_op jit(solution)/shard_map/kmc,mj->kjc/dot_general | solution.py:48
  412.5 24.6 %fusion.67 = (f32[1,32,25,1024]{3,2,1,0:T(8,128)}, f32[1,32,25,1024]{3,2,1,0:T(8,128)}, f32[1,32,25,1024]{3,2,1,0:T(8,128)}, f32[1,32,25,1024]{3,2,1,0:T(8,128)}) fusion(f32[1,32,25,1024]{3,1,2,0:T(8,128)} %get-tuple-element.25, f32[1,32,25,1024]{3,1,2,0:T(8,128)} %get-tuple-element.24, f32[25,32,1024]{2,0,1:T(8,128)} %fusion.130, ...), kind=kOutput, calls=%fused_computation.97 | convolution fusion | flops 483338816 | bytes 39059456 | tf_op jit(solution)/shard_map/kmc,mj->kjc/dot_general | solution.py:48
  468.0 34.5 %fusion.1 = f32[48,1024,32]{1,2,0:T(8,128)} fusion(f32[32,48]{0,1:T(8,128)S(1)} %fusion.151, f32[32,48]{0,1:T(8,128)S(1)} %get-tuple-element.34, f32[48,32,1024]{2,0,1:T(8,128)S(1)} %fusion.102, f32[48,32,1024]{2,0,1:T(8,128)S(1)} %fusion.98, f32[48,32,1024]{2,0,1:T(8,128)S(1)} %fusion.100, f32[48,32,1024]{2,0,1:T(8,128)} %fusion.96), kind=kOutput, calls=%fused_computation.9 | convolution fusion | flops 611858432 | bytes 31469568 | tf_op jit(solution)/shard_map/nk,kmc->cnm/dot_general | solution.py:83
  502.5 37.9 %multiply_bitcast_fusion = f32[1024,32,48]{0,1,2:T(8,128)} fusion(f32[48,1024,32]{1,2,0:T(8,128)} %fusion.1, f32[32,48]{0,1:T(8,128)S(1)} %fusion.151, f32[32,48]{0,1:T(8,128)S(1)} %get-tuple-element.34, f32[48,32,1024]{2,0,1:T(8,128)S(1)} %fusion.102, f32[48,32,1024]{2,0,1:T(8,128)S(1)} %fusion.98, f32[48,32,1024]{2,0,1:T(8,128)} %copy-done.2, ...), kind=kOutput, calls=%fused_computation.26 | convolution fusion | flops 615004160 | bytes 37761024 | tf_op jit(solution)/shard_map/nk,kmc->cnm/dot_general | solution.py:83
  549.4 42.9 %all-to-all-start = ((f32[16,64,768]{2,1,0:T(8,128)}), f32[16,64,768]{2,1,0:T(8,128)}, u32[]{:S(2)}, u32[]{:S(2)}) async-start(f32[16,64,768]{2,1,0:T(8,128)} %bitcast.46), calls=%async_computation | async-start | bytes 6291456 | tf_op jit(solution)/shard_map/all_to_all | solution.py:145
  623.8 29.8 %fusion.10 = f32[32,48,1024]{2,0,1:T(8,128)} fusion(f32[32,48]{0,1:T(8,128)S(1)} %fusion.151, f32[32,48]{0,1:T(8,128)S(1)} %get-tuple-element.34, f32[48,32,1024]{2,0,1:T(8,128)S(1)} %fusion.94, f32[48,32,1024]{2,0,1:T(8,128)S(1)} %fusion.90, f32[48,32,1024]{2,0,1:T(8,128)S(1)} %fusion.92, f32[48,32,1024]{2,0,1:T(8,128)} %fusion.88), kind=kOutput, calls=%fused_computation.19 | convolution fusion | flops 611858432 | bytes 31469568 | tf_op jit(solution)/shard_map/nk,kmc->nmc/dot_general | solution.py:87
  653.6 30.0 %fusion.7 = f32[32,48,1024]{2,0,1:T(8,128)} fusion(f32[32,48]{0,1:T(8,128)S(1)} %fusion.151, f32[32,48]{0,1:T(8,128)S(1)} %get-tuple-element.34, f32[48,32,1024]{2,0,1:T(8,128)S(1)} %fusion.94, f32[48,32,1024]{2,0,1:T(8,128)S(1)} %fusion.90, f32[48,32,1024]{2,0,1:T(8,128)S(1)} %fusion.92, f32[48,32,1024]{2,0,1:T(8,128)} %fusion.88), kind=kOutput, calls=%fused_computation.17 | convolution fusion | flops 611858432 | bytes 31469568 | tf_op jit(solution)/shard_map/nk,kmc->nmc/dot_general | solution.py:87
  (110 shorter events, 201.2 us)
Async XLA Ops:
  7.2 96.2 %all-gather.2.cloned.1.call-start = ((), (), s32[]{:S(2)}) async-start(), calls=%async_computation.1 | async-start | bytes 6684672 | tf_op jit(solution)/shard_map/all_gather | solution.py:109
  7.9 7.8 %collective-permute-start.2 = (f32[768,1024]{1,0:T(8,128)}, f32[768,1024]{1,0:T(8,128)S(1)}, u32[]{:S(2)}, u32[]{:S(2)}) collective-permute-start(f32[768,1024]{1,0:T(8,128)} %param.6), channel_id=1, source_target_pairs={{2,0},{4,2},{6,4},{8,6},{10,8},{12,10},{14,12},{16,14},{18,16},{20... | collective-permute-start | bytes 9437192 | tf_op jit(solution)/shard_map/ppermute | solution.py:13
  9.2 9.3 %collective-permute-start = (f32[768,1024]{1,0:T(8,128)}, f32[768,1024]{1,0:T(8,128)S(1)}, u32[]{:S(2)}, u32[]{:S(2)}) collective-permute-start(f32[768,1024]{1,0:T(8,128)} %param.5), channel_id=1, source_target_pairs={{0,2},{2,4},{4,6},{6,8},{8,10},{10,12},{12,14},{14,16},{16,18},{18... | collective-permute-start | bytes 9437192 | tf_op jit(solution)/shard_map/ppermute | solution.py:13
  18.5 21.3 %copy-start = (f32[1536,1024]{1,0:T(8,128)}, f32[1536,1024]{1,0:T(8,128)S(1)}, u32[]{:S(2)}) copy-start(f32[1536,1024]{1,0:T(8,128)S(1)} %pad_maximum_fusion.3) | copy-start | bytes 18874372
  39.8 63.6 %copy-start.8 = (f32[1024]{0:T(1024)S(1)}, f32[1024]{0:T(1024)}, u32[]{:S(2)}) copy-start(f32[1024]{0:T(1024)} %param.8) | copy-start | bytes 12292
  39.8 63.6 %copy-start.9 = (pred[1536]{0:T(1024)(128)(4,1)S(1)}, pred[1536]{0:T(1024)(128)(4,1)}, u32[]{:S(2)}) copy-start(pred[1536]{0:T(1024)(128)(4,1)} %constant.109.clone.1) | copy-start | bytes 4612
  190.0 10.7 %copy-start.1 = (f32[32,48,1024]{2,0,1:T(8,128)S(1)}, f32[32,48,1024]{2,0,1:T(8,128)}, u32[]{:S(2)}) copy-start(f32[32,48,1024]{2,0,1:T(8,128)} %get-tuple-element.13) | copy-start | bytes 18874372
  190.0 19.0 %slice-start.8 = ((s8[6291456]{0:T(1024)(128)(4,1)}), s8[4194304]{0:T(1024)(128)(4,1)S(1)}, s32[]{:S(2)}) async-start(s8[6291456]{0:T(1024)(128)(4,1)} %bitcast.305), calls=%async_computation.10 | async-start | bytes 8388608
  209.0 16.7 %slice-start.2 = ((s8[6291456]{0:T(1024)(128)(4,1)}), s8[4194304]{0:T(1024)(128)(4,1)S(1)}, s32[]{:S(2)}) async-start(s8[6291456]{0:T(1024)(128)(4,1)} %bitcast.297), calls=%async_computation.4 | async-start | bytes 8388608
  234.2 24.4 %slice-start = ((s8[6291456]{0:T(1024)(128)(4,1)}), s8[4194304]{0:T(1024)(128)(4,1)S(1)}, s32[]{:S(2)}) async-start(s8[6291456]{0:T(1024)(128)(4,1)} %bitcast.295), calls=%async_computation.2 | async-start | bytes 8388608
  242.3 16.2 %slice-start.1 = ((s8[6291456]{0:T(1024)(128)(4,1)}), s8[2097152]{0:T(1024)(128)(4,1)S(1)}, s32[]{:S(2)}) async-start(s8[6291456]{0:T(1024)(128)(4,1)} %bitcast.295), calls=%async_computation.3 | async-start | bytes 4194304
  247.0 11.6 %copy-start.5 = (f32[25,32,1024]{2,0,1:T(8,128)S(1)}, f32[25,32,1024]{2,0,1:T(8,128)}, u32[]{:S(2)}) copy-start(f32[25,32,1024]{2,0,1:T(8,128)} %fusion.38) | copy-start | bytes 9830404
  257.3 141.2 %collective-permute-start.3 = (f32[2,32,25,1024]{3,1,2,0:T(8,128)}, f32[2,32,25,1024]{3,1,2,0:T(8,128)}, u32[]{:S(2)}, u32[]{:S(2)}) collective-permute-start(f32[2,32,25,1024]{3,1,2,0:T(8,128)} %copy.136), channel_id=1, source_target_pairs={{2,0},{4,2},{6,4},{8,6},{10,8},{12,10},{14,12},{16,14},{18,16},{20... | collective-permute-start | bytes 19660808 | tf_op jit(solution)/shard_map/ppermute | solution.py:13
  266.7 8.8 %copy-start.4 = (f32[25,32,1024]{2,0,1:T(8,128)}, f32[25,32,1024]{2,0,1:T(8,128)S(1)}, u32[]{:S(2)}) copy-start(f32[25,32,1024]{2,0,1:T(8,128)S(1)} %fusion.121) | copy-start | bytes 9830404
  266.7 62.5 %slice-start.6 = ((s8[6291456]{0:T(1024)(128)(4,1)}), s8[2097152]{0:T(1024)(128)(4,1)S(1)}, s32[]{:S(2)}) async-start(s8[6291456]{0:T(1024)(128)(4,1)} %bitcast.301), calls=%async_computation.8 | async-start | bytes 4194304
  275.5 53.7 %slice-start.7 = ((s8[6291456]{0:T(1024)(128)(4,1)}), s8[4194304]{0:T(1024)(128)(4,1)S(1)}, s32[]{:S(2)}) async-start(s8[6291456]{0:T(1024)(128)(4,1)} %bitcast.301), calls=%async_computation.9 | async-start | bytes 8388608
  292.5 113.0 %collective-permute-start.1 = (f32[2,32,25,1024]{3,1,2,0:T(8,128)}, f32[2,32,25,1024]{3,1,2,0:T(8,128)}, u32[]{:S(2)}, u32[]{:S(2)}) collective-permute-start(f32[2,32,25,1024]{3,1,2,0:T(8,128)} %copy.120), channel_id=1, source_target_pairs={{0,2},{2,4},{4,6},{6,8},{8,10},{10,12},{12,14},{14,16},{16,18},{18... | collective-permute-start | bytes 19660808 | tf_op jit(solution)/shard_map/ppermute | solution.py:13
  329.2 16.5 %slice-start.4 = ((s8[6291456]{0:T(1024)(128)(4,1)}), s8[4194304]{0:T(1024)(128)(4,1)S(1)}, s32[]{:S(2)}) async-start(s8[6291456]{0:T(1024)(128)(4,1)} %bitcast.299), calls=%async_computation.6 | async-start | bytes 8388608
  337.3 8.5 %slice-start.5 = ((s8[6291456]{0:T(1024)(128)(4,1)}), s8[2097152]{0:T(1024)(128)(4,1)S(1)}, s32[]{:S(2)}) async-start(s8[6291456]{0:T(1024)(128)(4,1)} %bitcast.299), calls=%async_computation.7 | async-start | bytes 4194304
  345.8 16.6 %slice-start.14 = ((s8[6291456]{0:T(1024)(128)(4,1)}), s8[4194304]{0:T(1024)(128)(4,1)S(1)}, s32[]{:S(2)}) async-start(s8[6291456]{0:T(1024)(128)(4,1)} %bitcast.311), calls=%async_computation.16 | async-start | bytes 8388608
  353.8 8.5 %slice-start.15 = ((s8[6291456]{0:T(1024)(128)(4,1)}), s8[2097152]{0:T(1024)(128)(4,1)S(1)}, s32[]{:S(2)}) async-start(s8[6291456]{0:T(1024)(128)(4,1)} %bitcast.311), calls=%async_computation.17 | async-start | bytes 4194304
  353.9 16.9 %slice-start.10 = ((s8[6291456]{0:T(1024)(128)(4,1)}), s8[2097152]{0:T(1024)(128)(4,1)S(1)}, s32[]{:S(2)}) async-start(s8[6291456]{0:T(1024)(128)(4,1)} %bitcast.307), calls=%async_computation.12 | async-start | bytes 4194304
  398.4 14.1 %slice-start.12 = ((s8[6291456]{0:T(1024)(128)(4,1)}), s8[4194304]{0:T(1024)(128)(4,1)S(1)}, s32[]{:S(2)}) async-start(s8[6291456]{0:T(1024)(128)(4,1)} %bitcast.309), calls=%async_computation.14 | async-start | bytes 8388608
  549.4 141.5 %all-to-all-start = ((f32[16,64,768]{2,1,0:T(8,128)}), f32[16,64,768]{2,1,0:T(8,128)}, u32[]{:S(2)}, u32[]{:S(2)}) async-start(f32[16,64,768]{2,1,0:T(8,128)} %bitcast.46), calls=%async_computation | async-start | bytes 6291456 | tf_op jit(solution)/shard_map/all_to_all | solution.py:145
  (8 other events, 57.5 us)
Sparse Core Ops, SparseCore 0:
  10.3 93.1 all-gather.1
where the time goes:
time: 710 us; the launch traced here: 702 us
  matrix products  455 us (64%)
  starting transfers between devices  85.3 us (12%)
  waiting for transfers between devices  56.4 us (8%)
  local copies, waits for them, and re-layouts  52.3 us (7%)
  other arithmetic  38.3 us (5%)
  between operations  15 us (2%)
    dot_general x4, matrix products, forward_real(): jnp.einsum('kn,nmc->kmc', sin_first, grid_view, precision=PRECISE)  70.7 us
    dot_general x4, matrix products, forward_real(): jnp.einsum('kmc,mj->kjc', rot_real, cos_second, precision=PRECISE)  60.1 us
    all_gather x1, waiting for transfers between devices, local(): piece_rows = lax.all_gather(filter_rows, 'ctx', axis=0, tiled=True)  53.3 us
    all_to_all x1, starting transfers between devices, local(): lax.all_to_all(local_grad, 'ctx', split_axis=0, concat_axis=1, tiled=True)  42.9 us
    ppermute x4, starting transfers between devices, passed_along(): lax.ppermute(value, axis, [(source, source + steps) for source in range(i...  42.4 us
    dot_general x4, matrix products, forward_real(): jnp.einsum('kn,nmc->kmc', cos_first, grid_view, precision=PRECISE)  41.1 us
    dot_general x1, matrix products, inverse_real(): jnp.einsum('nk,kmc->cnm', sin_first, rot_imag, precision=PRECISE)  37.9 us
    dot_general x4, matrix products, forward_real(): jnp.einsum('kmc,mj->kjc', rot_imag, cos_second, precision=PRECISE)  34.9 us
  transfers between devices with their start and end apart: 6, of which 2 were waited for; matrix products, arithmetic and copies ran while one was open for 35% of the time, Pallas kernels for 0%

commit v1 on v0

--- a/solution.py
+++ b/solution.py
@@ -142,7 +142,10 @@
     outputs = lax.slice_in_dim(forward_time, block_len, 2 * block_len, axis=0)
     backward_time = inverse_real(totals[1], factors, True)
     local_grad = lax.slice_in_dim(backward_time, 0, block_len, axis=1)
-    input_grad = lax.all_to_all(local_grad, "ctx", split_axis=0, concat_axis=1, tiled=True)
+    input_grad = jnp.concatenate(
+        lax.all_to_all(jnp.stack(jnp.split(local_grad, lax.axis_size("ctx"), axis=0)), "ctx", 0, 0),
+        axis=1,
+    )
     return (outputs, input_grad)
 
 

time: 710 us -> 727 us (1.024)
  local copies, waits for them, and re-layouts: 52.3 us -> 69.7 us
    unnamed x52 -> x67, local copies, waits for them, and re-layouts: 0.47 us -> 13.4 us
  transfers between devices with their start and end apart: 6 -> 6, of which waited for: 2 -> 2; matrix products, arithmetic and copies ran while one was open for 35% -> 34% of each run, Pallas kernels for 0% -> 0%
where the time goes in v1:
time: 727 us; the launch traced here: 719 us
  matrix products  455 us (63%)
  starting transfers between devices  85.3 us (12%)
  local copies, waits for them, and re-layouts  69.7 us (10%)
  waiting for transfers between devices  56.4 us (8%)
  other arithmetic  38.3 us (5%)
  between operations  15 us (2%)
    dot_general x4, matrix products, forward_real(): jnp.einsum('kn,nmc->kmc', sin_first, grid_view, precision=PRECISE)  70.7 us
    dot_general x4, matrix products, forward_real(): jnp.einsum('kmc,mj->kjc', rot_real, cos_second, precision=PRECISE)  60.1 us
    all_gather x1, waiting for transfers between devices, local(): piece_rows = lax.all_gather(filter_rows, 'ctx', axis=0, tiled=True)  53.3 us
    all_to_all x1, starting transfers between devices, local(): lax.all_to_all(jnp.stack(jnp.split(local_grad, lax.axis_size('ctx'), axis...  42.9 us
    ppermute x4, starting transfers between devices, passed_along(): lax.ppermute(value, axis, [(source, source + steps) for source in range(i...  42.4 us
    dot_general x4, matrix products, forward_real(): jnp.einsum('kn,nmc->kmc', cos_first, grid_view, precision=PRECISE)  41.1 us
    dot_general x1, matrix products, inverse_real(): jnp.einsum('nk,kmc->cnm', sin_first, rot_imag, precision=PRECISE)  37.9 us
    dot_general x4, matrix products, forward_real(): jnp.einsum('kmc,mj->kjc', rot_imag, cos_second, precision=PRECISE)  34.9 us
  transfers between devices with their start and end apart: 6, of which 2 were waited for; matrix products, arithmetic and copies ran while one was open for 34% of the time, Pallas kernels for 0%

profile of v1, /device:TPU:0, one launch (start us, length us, event | category | flops | bytes accessed | tf_op | source)
XLA Modules:
  0.0 719.5 jit_solution(186891245333383068)
XLA Ops:
  19.7 10.0 %fusion.44 = f32[32,48,1024]{2,0,1:T(8,128)} fusion(f32[32,48,1024]{2,1,0:T(8,128)S(1)} %bitcast.380), kind=kOutput, calls=%fused_computation.69 | convolution fusion | flops 603995136 | bytes 12582912 | tf_op jit(solution)/shard_map/kn,nmc->kmc/dot_general | solution.py:43
  29.7 10.1 %fusion.46 = f32[32,48,1024]{2,0,1:T(8,128)} fusion(f32[32,48,1024]{2,1,0:T(8,128)S(1)} %bitcast.381), kind=kOutput, calls=%fused_computation.71 | convolution fusion | flops 603994112 | bytes 12582912 | tf_op jit(solution)/shard_map/kn,nmc->kmc/dot_general | solution.py:42
  39.8 10.3 %fusion.22 = f32[32,48,1024]{2,0,1:T(8,128)} fusion(f32[32,48,1024]{2,1,0:T(8,128)S(1)} %bitcast.366), kind=kOutput, calls=%fused_computation.47 | convolution fusion | flops 603994112 | bytes 12582912 | tf_op jit(solution)/shard_map/kn,nmc->kmc/dot_general | solution.py:42
  50.1 53.3 %all-gather.2.cloned.1.call-done = f32[1536,1024]{1,0:T(8,128)} async-done(((f32[96,1024]{1,0:T(8,128)}), f32[1536,1024]{1,0:T(8,128)}) %all-gather.2.cloned.1.call-update) | async-done | bytes 6291472 | tf_op jit(solution)/shard_map/all_gather | solution.py:109
  108.7 10.1 %fusion.32 = f32[32,48,1024]{2,0,1:T(8,128)} fusion(f32[32,48,1024]{2,1,0:T(8,128)S(1)} %bitcast.378), kind=kOutput, calls=%fused_computation.57 | convolution fusion | flops 603995136 | bytes 12582912 | tf_op jit(solution)/shard_map/kn,nmc->kmc/dot_general | solution.py:43
  118.7 10.4 %fusion.34 = f32[32,48,1024]{2,0,1:T(8,128)} fusion(f32[32,48,1024]{2,1,0:T(8,128)S(1)} %bitcast.379), kind=kOutput, calls=%fused_computation.59 | convolution fusion | flops 603994112 | bytes 12582912 | tf_op jit(solution)/shard_map/kn,nmc->kmc/dot_general | solution.py:42
  129.2 10.1 %fusion.56 = f32[32,48,1024]{2,0,1:T(8,128)} fusion(f32[32,48,1024]{2,1,0:T(8,128)S(1)} %bitcast.376), kind=kOutput, calls=%fused_computation.81 | convolution fusion | flops 603995136 | bytes 12582912 | tf_op jit(solution)/shard_map/kn,nmc->kmc/dot_general | solution.py:43
  139.2 10.3 %fusion.58 = f32[32,48,1024]{2,0,1:T(8,128)} fusion(f32[32,48,1024]{2,1,0:T(8,128)S(1)} %bitcast.377), kind=kOutput, calls=%fused_computation.83 | convolution fusion | flops 603994112 | bytes 12582912 | tf_op jit(solution)/shard_map/kn,nmc->kmc/dot_general | solution.py:42
  149.5 40.5 %multiply_subtract_fusion = (f32[32,48,1024]{2,0,1:T(8,128)}, f32[32,48,1024]{2,0,1:T(8,128)}, f32[32,48,1024]{2,0,1:T(8,128)}, f32[32,48,1024]{2,0,1:T(8,128)},...) fusion(f32[32,48,1024]{2,0,1:T(8,128)} %fusion.22, ...), kind=kOutput, calls=%fused_computation.28 | convolution fusion | flops 641743872 | bytes 100675584 | tf_op jit(solution)/shard_map/kn,nmc->kmc/dot_general | solution.py:43
  190.1 10.7 %fusion.12 = f32[25,32,1024]{2,0,1:T(8,128)S(1)} fusion(f32[32,48,1024]{2,0,1:T(8,128)} %get-tuple-element.15), kind=kOutput, calls=%fused_computation.37 | convolution fusion | flops 471870016 | bytes 9568256 | tf_op jit(solution)/shard_map/kmc,mj->kjc/dot_general | solution.py:51
  209.0 8.6 %fusion.38 = f32[25,32,1024]{2,0,1:T(8,128)} fusion(f32[32,48,1024]{2,0,1:T(8,128)S(1)} %bitcast.369), kind=kOutput, calls=%fused_computation.63 | convolution fusion | flops 471871200 | bytes 9568256 | tf_op jit(solution)/shard_map/kmc,mj->kjc/dot_general | solution.py:48
  247.0 10.3 %copy.156 = f32[2,32,25,1024]{3,1,2,0:T(8,128)} copy(f32[2,32,25,1024]{3,2,1,0:T(8,128)} %pad_maximum_fusion.1) | data formatting | bytes 13107200 | tf_op jit(solution)/shard_map/stack | solution.py:54
  266.7 8.8 %fusion.124 = f32[25,32,1024]{2,0,1:T(8,128)} fusion(f32[25,32,1024]{2,0,1:T(8,128)S(1)} %fusion.36, f32[32,48,1024]{2,0,1:T(8,128)S(1)} %bitcast.359), kind=kOutput, calls=%fused_computation.153 | convolution fusion | flops 472690400 | bytes 12845056 | tf_op jit(solution)/shard_map/kmc,mj->kjc/dot_general | solution.py:51
  282.6 9.9 %copy.140 = f32[2,32,25,1024]{3,1,2,0:T(8,128)} copy(f32[2,32,25,1024]{3,2,1,0:T(8,128)} %pad_maximum_fusion) | data formatting | bytes 13107200 | tf_op jit(solution)/shard_map/stack | solution.py:54
  292.5 36.6 %collective-permute-start.1 = (f32[2,32,25,1024]{3,1,2,0:T(8,128)}, f32[2,32,25,1024]{3,1,2,0:T(8,128)}, u32[]{:S(2)}, u32[]{:S(2)}) collective-permute-start(f32[2,32,25,1024]{3,1,2,0:T(8,128)} %copy.140), channel_id=1, source_target_pairs={{0,2},{2,4},{4,6},{6,8},{8,10},{10,12},{12,14},{14,16},{16,18},{18... | collective-permute-start | bytes 19660808 | tf_op jit(solution)/shard_map/ppermute | solution.py:13
  337.3 8.4 %fusion.50 = f32[25,32,1024]{2,0,1:T(8,128)} fusion(f32[32,48,1024]{2,0,1:T(8,128)S(1)} %bitcast.365), kind=kOutput, calls=%fused_computation.75 | convolution fusion | flops 471871200 | bytes 9568256 | tf_op jit(solution)/shard_map/kmc,mj->kjc/dot_general | solution.py:48
  353.9 8.5 %fusion.26 = f32[25,32,1024]{2,0,1:T(8,128)} fusion(f32[32,48,1024]{2,0,1:T(8,128)S(1)} %bitcast.363), kind=kOutput, calls=%fused_computation.51 | convolution fusion | flops 471871200 | bytes 9568256 | tf_op jit(solution)/shard_map/kmc,mj->kjc/dot_general | solution.py:48
  379.1 19.3 %fusion.81 = (f32[1,32,25,1024]{3,2,1,0:T(8,128)}, f32[1,32,25,1024]{3,2,1,0:T(8,128)}, f32[1,32,25,1024]{3,2,1,0:T(8,128)}, f32[1,32,25,1024]{3,2,1,0:T(8,128)}) fusion(f32[25,32,1024]{2,0,1:T(8,128)S(1)} %fusion.136, f32[25,32,1024]{2,0,1:T(8,128)} %copy-done.3, f32[25,32,1024]{2,0,1:T(8,128)} %fusion.118, f32[25,32,1024]{2,0,1:T(8,128)} %copy-done.4, ...), kind=kOutput, calls=%fused_computation.116 | convolution fusion | flops 483338816 | bytes 39059456 | tf_op jit(solution)/shard_map/kmc,mj->kjc/dot_general | solution.py:48
  412.5 24.6 %fusion.67 = (f32[1,32,25,1024]{3,2,1,0:T(8,128)}, f32[1,32,25,1024]{3,2,1,0:T(8,128)}, f32[1,32,25,1024]{3,2,1,0:T(8,128)}, f32[1,32,25,1024]{3,2,1,0:T(8,128)}) fusion(f32[1,32,25,1024]{3,1,2,0:T(8,128)} %get-tuple-element.27, f32[1,32,25,1024]{3,1,2,0:T(8,128)} %get-tuple-element.26, f32[25,32,1024]{2,0,1:T(8,128)} %fusion.130, ...), kind=kOutput, calls=%fused_computation.97 | convolution fusion | flops 483338816 | bytes 39059456 | tf_op jit(solution)/shard_map/kmc,mj->kjc/dot_general | solution.py:48
  468.0 34.5 %fusion.1 = f32[48,1024,32]{1,2,0:T(8,128)} fusion(f32[32,48]{0,1:T(8,128)S(1)} %fusion.167, f32[32,48]{0,1:T(8,128)S(1)} %get-tuple-element.36, f32[48,32,1024]{2,0,1:T(8,128)S(1)} %fusion.102, f32[48,32,1024]{2,0,1:T(8,128)S(1)} %fusion.98, f32[48,32,1024]{2,0,1:T(8,128)S(1)} %fusion.100, f32[48,32,1024]{2,0,1:T(8,128)} %fusion.96), kind=kOutput, calls=%fused_computation.9 | convolution fusion | flops 611858432 | bytes 31469568 | tf_op jit(solution)/shard_map/nk,kmc->cnm/dot_general | solution.py:83
  502.5 37.9 %multiply_bitcast_fusion = f32[1024,32,48]{0,1,2:T(8,128)} fusion(f32[48,1024,32]{1,2,0:T(8,128)} %fusion.1, f32[32,48]{0,1:T(8,128)S(1)} %fusion.167, f32[32,48]{0,1:T(8,128)S(1)} %get-tuple-element.36, f32[48,32,1024]{2,0,1:T(8,128)S(1)} %fusion.102, f32[48,32,1024]{2,0,1:T(8,128)S(1)} %fusion.98, f32[48,32,1024]{2,0,1:T(8,128)} %copy-done.2, ...), kind=kOutput, calls=%fused_computation.26 | convolution fusion | flops 615004160 | bytes 37761024 | tf_op jit(solution)/shard_map/nk,kmc->cnm/dot_general | solution.py:83
  566.8 42.9 %all-to-all-start = ((f32[16,64,768]{2,1,0:T(8,128)}), f32[16,64,768]{2,1,0:T(8,128)}, u32[]{:S(2)}, u32[]{:S(2)}) async-start(f32[16,64,768]{2,1,0:T(8,128)} %copy.164), calls=%async_computation | async-start | bytes 6291456 | tf_op jit(solution)/shard_map/all_to_all | solution.py:146
  641.1 29.8 %fusion.10 = f32[32,48,1024]{2,0,1:T(8,128)} fusion(f32[32,48]{0,1:T(8,128)S(1)} %fusion.167, f32[32,48]{0,1:T(8,128)S(1)} %get-tuple-element.36, f32[48,32,1024]{2,0,1:T(8,128)S(1)} %fusion.94, f32[48,32,1024]{2,0,1:T(8,128)S(1)} %fusion.90, f32[48,32,1024]{2,0,1:T(8,128)S(1)} %fusion.92, f32[48,32,1024]{2,0,1:T(8,128)} %fusion.88), kind=kOutput, calls=%fused_computation.19 | convolution fusion | flops 611858432 | bytes 31469568 | tf_op jit(solution)/shard_map/nk,kmc->nmc/dot_general | solution.py:87
  671.0 30.0 %fusion.7 = f32[32,48,1024]{2,0,1:T(8,128)} fusion(f32[32,48]{0,1:T(8,128)S(1)} %fusion.167, f32[32,48]{0,1:T(8,128)S(1)} %get-tuple-element.36, f32[48,32,1024]{2,0,1:T(8,128)S(1)} %fusion.94, f32[48,32,1024]{2,0,1:T(8,128)S(1)} %fusion.90, f32[48,32,1024]{2,0,1:T(8,128)S(1)} %fusion.92, f32[48,32,1024]{2,0,1:T(8,128)} %fusion.88), kind=kOutput, calls=%fused_computation.17 | convolution fusion | flops 611858432 | bytes 31469568 | tf_op jit(solution)/shard_map/nk,kmc->nmc/dot_general | solution.py:87
  (125 shorter events, 218.6 us)
Async XLA Ops:
  7.2 96.2 %all-gather.2.cloned.1.call-start = ((), (), s32[]{:S(2)}) async-start(), calls=%async_computation.1 | async-start | bytes 6684672 | tf_op jit(solution)/shard_map/all_gather | solution.py:109
  7.9 7.8 %collective-permute-start.2 = (f32[768,1024]{1,0:T(8,128)}, f32[768,1024]{1,0:T(8,128)S(1)}, u32[]{:S(2)}, u32[]{:S(2)}) collective-permute-start(f32[768,1024]{1,0:T(8,128)} %param.6), channel_id=1, source_target_pairs={{2,0},{4,2},{6,4},{8,6},{10,8},{12,10},{14,12},{16,14},{18,16},{20... | collective-permute-start | bytes 9437192 | tf_op jit(solution)/shard_map/ppermute | solution.py:13
  9.2 9.3 %collective-permute-start = (f32[768,1024]{1,0:T(8,128)}, f32[768,1024]{1,0:T(8,128)S(1)}, u32[]{:S(2)}, u32[]{:S(2)}) collective-permute-start(f32[768,1024]{1,0:T(8,128)} %param.5), channel_id=1, source_target_pairs={{0,2},{2,4},{4,6},{6,8},{8,10},{10,12},{12,14},{14,16},{16,18},{18... | collective-permute-start | bytes 9437192 | tf_op jit(solution)/shard_map/ppermute | solution.py:13
  18.5 21.3 %copy-start = (f32[1536,1024]{1,0:T(8,128)}, f32[1536,1024]{1,0:T(8,128)S(1)}, u32[]{:S(2)}) copy-start(f32[1536,1024]{1,0:T(8,128)S(1)} %pad_maximum_fusion.3) | copy-start | bytes 18874372
  39.8 63.6 %copy-start.8 = (f32[1024]{0:T(1024)S(1)}, f32[1024]{0:T(1024)}, u32[]{:S(2)}) copy-start(f32[1024]{0:T(1024)} %param.8) | copy-start | bytes 12292
  39.8 63.6 %copy-start.9 = (pred[1536]{0:T(1024)(128)(4,1)S(1)}, pred[1536]{0:T(1024)(128)(4,1)}, u32[]{:S(2)}) copy-start(pred[1536]{0:T(1024)(128)(4,1)} %constant.109.clone.1) | copy-start | bytes 4612
  190.0 10.7 %copy-start.1 = (f32[32,48,1024]{2,0,1:T(8,128)S(1)}, f32[32,48,1024]{2,0,1:T(8,128)}, u32[]{:S(2)}) copy-start(f32[32,48,1024]{2,0,1:T(8,128)} %get-tuple-element.15) | copy-start | bytes 18874372
  190.0 19.0 %slice-start.8 = ((s8[6291456]{0:T(1024)(128)(4,1)}), s8[4194304]{0:T(1024)(128)(4,1)S(1)}, s32[]{:S(2)}) async-start(s8[6291456]{0:T(1024)(128)(4,1)} %bitcast.368), calls=%async_computation.10 | async-start | bytes 8388608
  209.0 16.7 %slice-start.2 = ((s8[6291456]{0:T(1024)(128)(4,1)}), s8[4194304]{0:T(1024)(128)(4,1)S(1)}, s32[]{:S(2)}) async-start(s8[6291456]{0:T(1024)(128)(4,1)} %bitcast.360), calls=%async_computation.4 | async-start | bytes 8388608
  234.2 24.4 %slice-start = ((s8[6291456]{0:T(1024)(128)(4,1)}), s8[4194304]{0:T(1024)(128)(4,1)S(1)}, s32[]{:S(2)}) async-start(s8[6291456]{0:T(1024)(128)(4,1)} %bitcast.358), calls=%async_computation.2 | async-start | bytes 8388608
  242.3 16.2 %slice-start.1 = ((s8[6291456]{0:T(1024)(128)(4,1)}), s8[2097152]{0:T(1024)(128)(4,1)S(1)}, s32[]{:S(2)}) async-start(s8[6291456]{0:T(1024)(128)(4,1)} %bitcast.358), calls=%async_computation.3 | async-start | bytes 4194304
  247.0 11.6 %copy-start.5 = (f32[25,32,1024]{2,0,1:T(8,128)S(1)}, f32[25,32,1024]{2,0,1:T(8,128)}, u32[]{:S(2)}) copy-start(f32[25,32,1024]{2,0,1:T(8,128)} %fusion.38) | copy-start | bytes 9830404
  257.3 141.2 %collective-permute-start.3 = (f32[2,32,25,1024]{3,1,2,0:T(8,128)}, f32[2,32,25,1024]{3,1,2,0:T(8,128)}, u32[]{:S(2)}, u32[]{:S(2)}) collective-permute-start(f32[2,32,25,1024]{3,1,2,0:T(8,128)} %copy.156), channel_id=1, source_target_pairs={{2,0},{4,2},{6,4},{8,6},{10,8},{12,10},{14,12},{16,14},{18,16},{20... | collective-permute-start | bytes 19660808 | tf_op jit(solution)/shard_map/ppermute | solution.py:13
  266.7 8.8 %copy-start.4 = (f32[25,32,1024]{2,0,1:T(8,128)}, f32[25,32,1024]{2,0,1:T(8,128)S(1)}, u32[]{:S(2)}) copy-start(f32[25,32,1024]{2,0,1:T(8,128)S(1)} %fusion.121) | copy-start | bytes 9830404
  266.7 62.5 %slice-start.6 = ((s8[6291456]{0:T(1024)(128)(4,1)}), s8[2097152]{0:T(1024)(128)(4,1)S(1)}, s32[]{:S(2)}) async-start(s8[6291456]{0:T(1024)(128)(4,1)} %bitcast.364), calls=%async_computation.8 | async-start | bytes 4194304
  275.5 53.7 %slice-start.7 = ((s8[6291456]{0:T(1024)(128)(4,1)}), s8[4194304]{0:T(1024)(128)(4,1)S(1)}, s32[]{:S(2)}) async-start(s8[6291456]{0:T(1024)(128)(4,1)} %bitcast.364), calls=%async_computation.9 | async-start | bytes 8388608
  292.5 113.0 %collective-permute-start.1 = (f32[2,32,25,1024]{3,1,2,0:T(8,128)}, f32[2,32,25,1024]{3,1,2,0:T(8,128)}, u32[]{:S(2)}, u32[]{:S(2)}) collective-permute-start(f32[2,32,25,1024]{3,1,2,0:T(8,128)} %copy.140), channel_id=1, source_target_pairs={{0,2},{2,4},{4,6},{6,8},{8,10},{10,12},{12,14},{14,16},{16,18},{18... | collective-permute-start | bytes 19660808 | tf_op jit(solution)/shard_map/ppermute | solution.py:13
  329.2 16.5 %slice-start.4 = ((s8[6291456]{0:T(1024)(128)(4,1)}), s8[4194304]{0:T(1024)(128)(4,1)S(1)}, s32[]{:S(2)}) async-start(s8[6291456]{0:T(1024)(128)(4,1)} %bitcast.362), calls=%async_computation.6 | async-start | bytes 8388608
  337.3 8.5 %slice-start.5 = ((s8[6291456]{0:T(1024)(128)(4,1)}), s8[2097152]{0:T(1024)(128)(4,1)S(1)}, s32[]{:S(2)}) async-start(s8[6291456]{0:T(1024)(128)(4,1)} %bitcast.362), calls=%async_computation.7 | async-start | bytes 4194304
  345.8 16.6 %slice-start.14 = ((s8[6291456]{0:T(1024)(128)(4,1)}), s8[4194304]{0:T(1024)(128)(4,1)S(1)}, s32[]{:S(2)}) async-start(s8[6291456]{0:T(1024)(128)(4,1)} %bitcast.374), calls=%async_computation.16 | async-start | bytes 8388608
  353.8 8.5 %slice-start.15 = ((s8[6291456]{0:T(1024)(128)(4,1)}), s8[2097152]{0:T(1024)(128)(4,1)S(1)}, s32[]{:S(2)}) async-start(s8[6291456]{0:T(1024)(128)(4,1)} %bitcast.374), calls=%async_computation.17 | async-start | bytes 4194304
  353.8 16.9 %slice-start.10 = ((s8[6291456]{0:T(1024)(128)(4,1)}), s8[2097152]{0:T(1024)(128)(4,1)S(1)}, s32[]{:S(2)}) async-start(s8[6291456]{0:T(1024)(128)(4,1)} %bitcast.370), calls=%async_computation.12 | async-start | bytes 4194304
  398.4 14.1 %slice-start.12 = ((s8[6291456]{0:T(1024)(128)(4,1)}), s8[4194304]{0:T(1024)(128)(4,1)S(1)}, s32[]{:S(2)}) async-start(s8[6291456]{0:T(1024)(128)(4,1)} %bitcast.372), calls=%async_computation.14 | async-start | bytes 8388608
  566.8 141.6 %all-to-all-start = ((f32[16,64,768]{2,1,0:T(8,128)}), f32[16,64,768]{2,1,0:T(8,128)}, u32[]{:S(2)}, u32[]{:S(2)}) async-start(f32[16,64,768]{2,1,0:T(8,128)} %copy.164), calls=%async_computation | async-start | bytes 6291456 | tf_op jit(solution)/shard_map/all_to_all | solution.py:146
  (8 other events, 57.5 us)
Sparse Core Ops, SparseCore 0:
  10.3 93.1 all-gather.1
